TPU v7x, 32 devices: a whole 2x2x4 slice. The times are simulated.
32 devices in a mesh: head: 8 (over z, y), dp: 4 (over x, core).
Axes of the slice: x: 2, y: 2, z: 4, core: 2. Of those that a mesh axis runs over, the one named last changes fastest.
Arguments:
- attn_out: bfloat16 [1024, 8192], P('dp', 'head'), may hold values from -6 to 6
- head_mask: int32 [64], P('head'), may hold values from 0 to 1, as said below
- gate_scale: float32 [64], P('head'), may hold values from 0.25 to 2
- w_out: bfloat16 [8192, 8192], P('head', 'dp'), may hold values from -0.09375 to 0.09375
- grad_out: bfloat16 [1024, 8192], P(('dp', 'head')), may hold values from -6 to 6
Outputs:
- proj_out: bfloat16 [1024, 8192], P(('dp', 'head'))
- grad_attn: bfloat16 [1024, 8192], P('dp', 'head')
- grad_w: float32 [8192, 8192], P('head', 'dp')
Inputs may be any that keep to these rules, and one draw needn't show every extreme that they name: `head_mask`: exactly 32 heads are live.
All inputs are finite; a program needn't handle non-finite values.
Results may differ from a plain program's by a relative error of at most 0.0051.
Values may be sent and summed in bfloat16 or wider, within the bound.
A program may use at most 128 MiB of HBM per device.

v0:
```python
import jax
import jax.numpy as jnp
from jax import lax
from jax.sharding import PartitionSpec as P


def shards(attn_out, head_mask, gate_scale, w_out, grad_out):
    gate_vals = head_mask.astype(jnp.float32) * gate_scale
    width_each = attn_out.shape[1] // gate_vals.shape[0]
    col_gate = jnp.repeat(gate_vals, width_each)
    gated = (attn_out.astype(jnp.float32) * col_gate[None, :]).astype(jnp.bfloat16)
    weight_rows = lax.all_gather(w_out, "dp", axis=1, tiled=True)
    proj_out = lax.psum_scatter(
        jnp.dot(gated, weight_rows, preferred_element_type=jnp.float32),
        "head",
        scatter_dimension=0,
        tiled=True,
    ).astype(jnp.bfloat16)
    grad_full = lax.all_gather(grad_out, "head", axis=0, tiled=True)
    back_proj = lax.dot_general(
        grad_full, weight_rows, (((1,), (1,)), ((), ())), preferred_element_type=jnp.float32
    )
    grad_attn = (back_proj * col_gate[None, :]).astype(jnp.bfloat16)
    grad_local = lax.dot_general(
        gated, grad_full, (((0,), (0,)), ((), ())), preferred_element_type=jnp.float32
    )
    grad_w = lax.psum_scatter(grad_local, "dp", scatter_dimension=1, tiled=True)
    return (proj_out, grad_attn, grad_w)


def solution(mesh):
    return jax.shard_map(
        shards,
        mesh=mesh,
        in_specs=(P("dp", "head"), P("head"), P("head"), P("head", "dp"), P(("dp", "head"), None)),
        out_specs=(P(("dp", "head"), None), P("dp", "head"), P("head", "dp")),
        check_vma=False,
    )
```

profile of v0, /device:TPU:0, one launch (start us, length us, event | category | flops | bytes accessed | tf_op | source)
XLA Modules:
  0.0 583.7 jit_solution(12137804477661444461)
XLA Ops:
  7.2 0.0 all-gather.3.cloned.1.call-start
  7.2 0.7 all-gather.3.cloned.1.call-update
  7.9 0.0 all-gather.5.cloned.1.call-start
  7.9 0.7 all-gather.5.cloned.1.call-update
  8.6 0.0 reduce-scatter.3.cloned.1.call-start
  8.7 0.7 convert_multiply_fusion
  9.4 0.1 broadcast_bitcast_fusion
  9.4 108.7 %all-gather.3.cloned.1.call-done = bf16[1024,8192]{1,0:T(8,128)(2,1)} async-done(((bf16[1024,2048]{1,0:T(8,128)(2,1)}), bf16[1024,8192]{1,0:T(8,128)(2,1)}) %all-gather.3.cloned.1.call-update) | async-done | bytes 16777232 | tf_op jit(solution)/shard_map/all_gather | solution.py:12
  118.2 13.7 %fusion.2 = f32[256,8192]{1,0:T(8,128)} fusion(bf16[1024,8192]{1,0:T(8,128)(2,1)} %all-gather.3.cloned.1.call-done, bf16[256,1024]{1,0:T(8,128)(2,1)} %param.5, f32[1024]{0:T(1024)S(1)} %broadcast_bitcast_fusion), kind=kOutput, calls=%fused_computation.4 | convolution fusion | flops 4295753728 | bytes 25694208 | tf_op jit(solution)/shard_map/dot_general | solution.py:14
  131.9 0.0 copy-start
  131.9 0.0 reduce-scatter.3.cloned.1.call-update
  131.9 0.0 reduce-scatter.5.cloned.1.call-start
  131.9 61.2 %all-gather.5.cloned.1.call-done = bf16[256,8192]{1,0:T(8,128)(2,1)} async-done(((bf16[32,8192]{1,0:T(8,128)(2,1)}), bf16[256,8192]{1,0:T(8,128)(2,1)}) %all-gather.5.cloned.1.call-update) | async-done | bytes 4194320 | tf_op jit(solution)/shard_map/all_gather | solution.py:19
  193.1 0.0 copy-done
  193.1 15.9 %fusion.1 = f32[1024,8192]{1,0:T(8,128)} fusion(bf16[256,8192]{1,0:T(8,128)(2,1)} %all-gather.5.cloned.1.call-done, bf16[256,1024]{1,0:T(8,128)(2,1)S(1)} %copy-done, f32[1024]{0:T(1024)S(1)} %broadcast_bitcast_fusion), kind=kOutput, calls=%fused_computation.3 | convolution fusion | flops 4295753728 | bytes 38277120 | tf_op jit(solution)/shard_map/dot_general | solution.py:24
  209.0 0.0 reduce-scatter.5.cloned.1.call-update
  209.1 12.5 %fusion = bf16[256,1024]{1,0:T(8,128)(2,1)} fusion(bf16[256,8192]{1,0:T(8,128)(2,1)} %all-gather.5.cloned.1.call-done, bf16[1024,8192]{1,0:T(8,128)(2,1)} %all-gather.3.cloned.1.call-done, f32[1024]{0:T(1024)S(1)} %broadcast_bitcast_fusion), kind=kOutput, calls=%fused_computation.1 | convolution fusion | flops 4295491584 | bytes 21499904 | tf_op jit(solution)/shard_map/dot_general | solution.py:20
  221.5 121.3 %reduce-scatter.3.cloned.1.call-done = f32[32,8192]{1,0:T(8,128)} async-done(((f32[256,8192]{1,0:T(8,128)}), f32[32,8192]{1,0:T(8,128)}) %reduce-scatter.3.cloned.1.call-update) | async-done | bytes 1048592 | tf_op jit(solution)/shard_map/reduce_scatter | solution.py:13
  342.8 2.1 convert_element_type.18
  344.9 232.3 %reduce-scatter.5.cloned.1.call-done = f32[1024,2048]{1,0:T(8,128)} async-done(((f32[1024,8192]{1,0:T(8,128)}), f32[1024,2048]{1,0:T(8,128)}) %reduce-scatter.5.cloned.1.call-update) | async-done | bytes 8388624 | tf_op jit(solution)/shard_map/reduce_scatter | solution.py:27
Async XLA Ops:
  7.2 111.0 %all-gather.3.cloned.1.call-start = ((), (), s32[]{:S(2)}) async-start(), calls=%async_computation.2 | async-start | bytes 20971520 | tf_op jit(solution)/shard_map/all_gather | solution.py:12
  7.9 185.2 %all-gather.5.cloned.1.call-start = ((), (), s32[]{:S(2)}) async-start(), calls=%async_computation.4 | async-start | bytes 4718592 | tf_op jit(solution)/shard_map/all_gather | solution.py:19
  8.6 334.2 %reduce-scatter.3.cloned.1.call-start = ((), (), s32[]{:S(2)}) async-start(), calls=%async_computation.3 | async-start | bytes 9437184 | tf_op jit(solution)/shard_map/reduce_scatter | solution.py:13
  131.9 61.3 %copy-start = (bf16[256,1024]{1,0:T(8,128)(2,1)S(1)}, bf16[256,1024]{1,0:T(8,128)(2,1)}, u32[]{:S(2)}) copy-start(bf16[256,1024]{1,0:T(8,128)(2,1)} %param.5) | copy-start | bytes 1572868
  131.9 445.3 %reduce-scatter.5.cloned.1.call-start = ((), (), s32[]{:S(2)}) async-start(), calls=%async_computation.5 | async-start | bytes 41943040 | tf_op jit(solution)/shard_map/reduce_scatter | solution.py:27
Sparse Core Ops, SparseCore 0:
  9.5 108.6 all-gather.2
  120.3 72.7 all-gather.4
  196.8 145.9 reduce-scatter.2
  345.8 231.3 reduce-scatter.4
where the time goes:
time: 584 us
  waiting for transfers between devices  525 us (90%)
  matrix products  42.1 us (7%)
  between operations  13.8 us (2%)
    reduce_scatter x1, waiting for transfers between devices, shards(): grad_w = lax.psum_scatter(grad_local, 'dp', scatter_dimension=1, tiled=True)  232 us
    reduce_scatter x1, waiting for transfers between devices, shards(): lax.psum_scatter(jnp.dot(gated, weight_rows, preferred_element_type=jnp.f...  121 us
    all_gather x1, waiting for transfers between devices, shards(): weight_rows = lax.all_gather(w_out, 'dp', axis=1, tiled=True)  109 us
    all_gather x1, waiting for transfers between devices, shards(): grad_full = lax.all_gather(grad_out, 'head', axis=0, tiled=True)  61.2 us
    dot_general x1, matrix products, shards(): lax.dot_general(gated, grad_full, (((0,), (0,)), ((), ())), preferred_ele...  15.9 us
    dot_general x1, matrix products, shards(): jnp.dot(gated, weight_rows, preferred_element_type=jnp.float32)  13.7 us
    dot_general x1, matrix products, shards(): lax.dot_general(grad_full, weight_rows, (((1,), (1,)), ((), ())), preferr...  12.5 us
  transfers between devices with their start and end apart: 4, of which 4 were waited for; matrix products, arithmetic and copies ran while one was open for 8% of the time, Pallas kernels for 0%

commit v1 on v0

v1 whole, which is shorter than its diff:
```python
import jax
import jax.numpy as jnp
from jax import lax
from jax.sharding import PartitionSpec as P


def shards(attn_out, head_mask, gate_scale, w_out, grad_out):
    n_dp, n_head = lax.axis_size("dp"), lax.axis_size("head")
    gate_vals = head_mask.astype(jnp.float32) * gate_scale
    width_each = attn_out.shape[1] // gate_vals.shape[0]
    col_gate = jnp.repeat(gate_vals, width_each)
    gated = (attn_out.astype(jnp.float32) * col_gate[None, :]).astype(jnp.bfloat16)
    rows, cols = grad_out.shape[0], w_out.shape[1]
    mine = lax.all_to_all(grad_out, "dp", 1, 0, tiled=True)
    every = lax.all_gather(mine.reshape(n_dp, rows, cols), "head", axis=1)
    grad_cols = every.reshape(n_dp * n_head * rows, cols)
    gated_all = lax.all_gather(gated, "dp", axis=0, tiled=True)
    part = jnp.dot(gated_all, w_out, preferred_element_type=jnp.float32).astype(jnp.bfloat16)
    summed = lax.psum_scatter(part.reshape(n_dp, n_head, rows, cols), "head", scatter_dimension=1, tiled=False)
    proj_out = lax.all_to_all(summed.reshape(n_dp * rows, cols), "dp", 0, 1, tiled=True)
    back = lax.dot_general(grad_cols, w_out, (((1,), (1,)), ((), ())), preferred_element_type=jnp.float32)
    back = lax.psum_scatter(back.astype(jnp.bfloat16), "dp", scatter_dimension=0, tiled=True)
    grad_attn = (back.astype(jnp.float32) * col_gate[None, :]).astype(jnp.bfloat16)
    grad_w = lax.dot_general(gated_all, grad_cols, (((0,), (0,)), ((), ())), preferred_element_type=jnp.float32)
    return (proj_out, grad_attn, grad_w)


def solution(mesh):
    return jax.shard_map(
        shards,
        mesh=mesh,
        in_specs=(P("dp", "head"), P("head"), P("head"), P("head", "dp"), P(("dp", "head"), None)),
        out_specs=(P(("dp", "head"), None), P("dp", "head"), P("head", "dp")),
        check_vma=False,
    )
```

time: 584 us -> 352 us (0.60)
  waiting for transfers between devices: 525 us -> 281 us
  matrix products: 42.1 us -> 24.1 us
  local copies, waits for them, and re-layouts: 0.08 us -> 13.6 us
  blocking collectives: 0 us -> 12.9 us
    reduce_scatter x2 -> x1, waiting for transfers between devices: 354 us -> 29.7 us  [shards(): lax.psum_scatter(back.astype(jnp.bfloat16), 'dp', scatter_dimension=0, ti...]
    unnamed x4 -> x5, waiting for transfers between devices: 1.41 us -> 155 us
    all_gather x2, waiting for transfers between devices: 170 us -> 95.9 us  [the longest x1 73.2 us: shards(): every = lax.all_gather(mine.reshape(n_dp, rows, cols), 'head', axis=1)]
    dot_general x3, matrix products: 42.1 us -> 24.1 us  [the longest x1 9.33 us: shards(): jnp.dot(gated_all, w_out, preferred_element_type=jnp.float32)]
    all_to_all x0 -> x1, blocking collectives: none -> 12.9 us  [shards(): mine = lax.all_to_all(grad_out, 'dp', 1, 0, tiled=True)]
  transfers between devices with their start and end apart: 4 -> 5, of which waited for: 4 -> 4; matrix products, arithmetic and copies ran while one was open for 8% -> 3% of each run, Pallas kernels for 0% -> 0%
where the time goes in v1:
time: 352 us; the launch traced here: 351 us
  waiting for transfers between devices  281 us (80%)
  matrix products  24.1 us (7%)
  between operations  13.8 us (4%)
  local copies, waits for them, and re-layouts  13.6 us (4%)
  blocking collectives  12.9 us (4%)
  starting transfers between devices  3.64 us (1%)
    unnamed x5, waiting for transfers between devices  155 us
    all_gather x1, waiting for transfers between devices, shards(): every = lax.all_gather(mine.reshape(n_dp, rows, cols), 'head', axis=1)  73.2 us
    reduce_scatter x1, waiting for transfers between devices, shards(): lax.psum_scatter(back.astype(jnp.bfloat16), 'dp', scatter_dimension=0, ti...  29.7 us
    all_gather x1, waiting for transfers between devices, shards(): gated_all = lax.all_gather(gated, 'dp', axis=0, tiled=True)  22.7 us
    all_to_all x1, blocking collectives, shards(): mine = lax.all_to_all(grad_out, 'dp', 1, 0, tiled=True)  12.9 us
    dot_general x1, matrix products, shards(): jnp.dot(gated_all, w_out, preferred_element_type=jnp.float32)  9.33 us
    dot_general x1, matrix products, shards(): lax.dot_general(gated_all, grad_cols, (((0,), (0,)), ((), ())), preferred...  9.02 us
  transfers between devices with their start and end apart: 5, of which 4 were waited for; matrix products, arithmetic and copies ran while one was open for 3% of the time, Pallas kernels for 0%

profile of v1, /device:TPU:0, one launch (start us, length us, event | category | flops | bytes accessed | tf_op | source)
XLA Modules:
  0.0 351.2 jit_solution(4821539071174276159)
XLA Ops:
  7.2 0.0 all-gather.6.cloned.1.call-start
  7.2 1.1 copy.24
  8.3 12.9 %all_to_all.35 = bf16[32,4,2048]{2,0,1:T(8,128)(2,1)S(1)} all-to-all(bf16[32,4,2048]{2,0,1:T(8,128)(2,1)S(1)} %bitcast.32), channel_id=1, replica_groups=mesh['head'=8,'dp'=4] {'dp'}, dimensions={1} | all-to-all | bytes 1048576 | tf_op jit(solution)/shard_map/all_to_all | solution.py:14
  21.1 1.2 copy.17
  22.3 0.0 all-gather.6.cloned.1.call-update
  22.4 0.0 reduce-scatter.5.cloned.1.call-start
  22.4 73.2 %all-gather.6.cloned.1.call-done = bf16[4,256,2048]{2,0,1:T(4,128)(2,1)} async-done(((bf16[4,32,2048]{2,0,1:T(4,128)(2,1)}), bf16[4,256,2048]{2,0,1:T(4,128)(2,1)}) %all-gather.6.cloned.1.call-update) | async-done | bytes 4194320 | tf_op jit(solution)/shard_map/all_gather | solution.py:15
  95.6 0.0 copy-start.2
  95.6 4.6 %copy.18 = bf16[4,256,2048]{2,1,0:T(8,128)(2,1)S(1)} copy(bf16[4,256,2048]{2,0,1:T(4,128)(2,1)} %all-gather.6.cloned.1.call-done) | data formatting | bytes 8388608 | tf_op jit(solution)/shard_map/all_gather | solution.py:15
  100.3 0.0 copy-start
  100.3 2.0 copy-done
  102.2 0.0 copy-done.2
  102.2 0.0 copy-start.4
  102.2 0.0 copy-start.5
  102.3 0.0 copy-start.1
  102.3 5.7 %convolution_convert_fusion.1 = bf16[1024,1024]{1,0:T(8,128)(2,1)} fusion(bf16[1024,2048]{1,0:T(8,128)(2,1)S(1)} %bitcast.27, bf16[1024,2048]{1,0:T(8,128)(2,1)S(1)} %copy-done.2), kind=kOutput, calls=%fused_computation.1 | convolution fusion | flops 4296015872 | bytes 10485760 | tf_op jit(solution)/shard_map/dot_general | solution.py:21
  108.0 0.0 reduce-scatter.5.cloned.1.call-update
  108.0 0.0 all-gather.4.cloned.1.call-start
  108.1 0.0 copy-done.4
  108.1 0.0 copy-done.5
  108.1 0.1 broadcast_bitcast_fusion
  108.2 29.7 %reduce-scatter.5.cloned.1.call-done = bf16[256,1024]{1,0:T(8,128)(2,1)} async-done(((bf16[1024,1024]{1,0:T(8,128)(2,1)}), bf16[256,1024]{1,0:T(8,128)(2,1)}) %reduce-scatter.5.cloned.1.call-update) | async-done | bytes 524304 | tf_op jit(solution)/shard_map/reduce_scatter | solution.py:22
  137.9 0.0 copy-done.1
  137.9 2.3 multiply_convert_fusion
  140.1 0.0 all-gather.4.cloned.1.call-update
  140.1 0.0 all-reduce.3.cloned.1.call-start
  140.2 22.7 %all-gather.4.cloned.1.call-done = bf16[1024,1024]{1,0:T(8,128)(2,1)} async-done(((bf16[256,1024]{1,0:T(8,128)(2,1)}), bf16[1024,1024]{1,0:T(8,128)(2,1)}) %all-gather.4.cloned.1.call-update) | async-done | bytes 2097168 | tf_op jit(solution)/shard_map/all_gather | solution.py:17
  162.9 9.3 %convolution_convert_fusion = bf16[1024,2048]{1,0:T(8,128)(2,1)} fusion(bf16[1024,1024]{1,0:T(8,128)(2,1)} %all-gather.4.cloned.1.call-done, bf16[1024,2048]{1,0:T(8,128)(2,1)} %param.8), kind=kOutput, calls=%fused_computation | convolution fusion | flops 4297064448 | bytes 10485760 | tf_op jit(solution)/shard_map/dot_general | solution.py:18
  172.2 0.0 copy-start.6
  172.2 0.0 copy-start.3
  172.2 0.0 all-reduce.3.cloned.1.call-update
  172.2 0.6 copy-done.6
  172.8 0.7 dynamic-slice
  173.5 155.3 %all-reduce.3.cloned.1.call-done = bf16[4,8,32,2048]{3,2,1,0:T(8,128)(2,1)} async-done(((bf16[4,8,32,2048]{3,2,1,0:T(8,128)(2,1)}), bf16[4,8,32,2048]{3,2,1,0:T(8,128)(2,1)}) %all-reduce.3.cloned.1.call-update) | async-done | bytes 4194320
  328.8 2.6 dynamic-slice_bitcast_fusion
  331.3 3.5 all-to-all-start
  334.8 0.0 copy-done.3
  334.8 9.0 %fusion = f32[1024,2048]{1,0:T(8,128)} fusion(bf16[1024,1024]{1,0:T(8,128)(2,1)S(1)} %copy-done.3, bf16[1024,2048]{1,0:T(8,128)(2,1)} %bitcast.28), kind=kOutput, calls=%fused_computation.8 | convolution fusion | flops 4294967296 | bytes 14680064 | tf_op jit(solution)/shard_map/dot_general | solution.py:24
  343.8 0.0 all-to-all-done
  343.8 0.8 copy.22
  (1 shorter events, 0.0 us)
Async XLA Ops:
  7.2 88.5 %all-gather.6.cloned.1.call-start = ((), (), s32[]{:S(2)}) async-start(), calls=%async_computation.5 | async-start | bytes 4718592 | tf_op jit(solution)/shard_map/all_gather | solution.py:15
  22.4 115.5 %reduce-scatter.5.cloned.1.call-start = ((), (), s32[]{:S(2)}) async-start(), calls=%async_computation.4 | async-start | bytes 2621440 | tf_op jit(solution)/shard_map/reduce_scatter | solution.py:22
  95.6 6.6 %copy-start.2 = (bf16[1024,2048]{1,0:T(8,128)(2,1)S(1)}, bf16[1024,2048]{1,0:T(8,128)(2,1)}, u32[]{:S(2)}) copy-start(bf16[1024,2048]{1,0:T(8,128)(2,1)} %param.8) | copy-start | bytes 12582916
  100.3 2.0 copy-start
  102.2 5.8 %copy-start.4 = (f32[8]{0:T(128)S(1)}, f32[8]{0:T(128)}, u32[]{:S(2)}) copy-start(f32[8]{0:T(128)} %param.7) | copy-start | bytes 100
  102.2 5.8 %copy-start.5 = (s32[8]{0:T(128)S(1)}, s32[8]{0:T(128)}, u32[]{:S(2)}) copy-start(s32[8]{0:T(128)} %param.6) | copy-start | bytes 100
  102.3 35.6 %copy-start.1 = (bf16[256,1024]{1,0:T(8,128)(2,1)S(1)}, bf16[256,1024]{1,0:T(8,128)(2,1)}, u32[]{:S(2)}) copy-start(bf16[256,1024]{1,0:T(8,128)(2,1)} %param.5) | copy-start | bytes 1572868
  108.0 54.8 %all-gather.4.cloned.1.call-start = ((), (), s32[]{:S(2)}) async-start(), calls=%async_computation.3 | async-start | bytes 2621440 | tf_op jit(solution)/shard_map/all_gather | solution.py:17
  140.1 188.6 %all-reduce.3.cloned.1.call-start = ((), (), s32[]{:S(2)}) async-start(), calls=%async_computation.6 | async-start | bytes 8388608
  172.2 0.7 copy-start.6
  172.2 162.6 %copy-start.3 = (bf16[1024,1024]{1,0:T(8,128)(2,1)S(1)}, bf16[1024,1024]{1,0:T(8,128)(2,1)}, u32[]{:S(2)}) copy-start(bf16[1024,1024]{1,0:T(8,128)(2,1)} %all-gather.4.cloned.1.call-done) | copy-start | bytes 6291460
  331.3 12.5 %all-to-all-start = ((bf16[4,32,2048]{2,1,0:T(8,128)(2,1)}), bf16[4,32,2048]{2,1,0:T(8,128)(2,1)S(1)}, u32[]{:S(2)}, u32[]{:S(2)}) async-start(bf16[4,32,2048]{2,1,0:T(8,128)(2,1)} %dynamic-slice_bitcast_fusion), calls=%async_computation | async-start | bytes 1048576 | tf_op jit(solution)/shard_map/all_to_all | solution.py:20
Sparse Core Ops, SparseCore 0:
  22.5 73.0 all-gather.5
  108.1 29.6 reduce-scatter.4
  140.3 22.5 all-gather.3
  172.3 156.3 all-reduce.2

commit v2 on v1

--- a/solution.py
+++ b/solution.py
@@ -1,7 +1,266 @@
+import functools
+
 import jax
 import jax.numpy as jnp
 from jax import lax
+from jax.experimental import pallas as pl
+from jax.experimental.pallas import tpu as pltpu
 from jax.sharding import PartitionSpec as P
+
+MESH = pl.DeviceIdType.MESH
+F32, BF16 = jnp.float32, jnp.bfloat16
+TILE = 256
+VMEM_LIMIT = 62 * 1024 * 1024
+
+
+def kernel(nh, nd, attn, gate, grad, w_hbm, proj, gattn, gw_hbm,
+           blocks, gated, w, g, ps, po, ry, sz, rz, fin, pj, bs, bo, br, bs2, br2, stage,
+           ssem, rsem, lsem, osem):
+    na, nx = nh // 2, nd // 2
+    h, d = lax.axis_index("head"), lax.axis_index("dp")
+    a, b = h // 2, h % 2
+    x, c = d // 2, d % 2
+    rows, cols = fin.shape[1:]
+    width = attn.shape[1]
+    other = a * 2 + 1 - b
+    sibling = x * 2 + 1 - c
+    copies = []
+
+    def send(src, dst, hh, dd):
+        i = len(copies)
+        copy = pltpu.make_async_remote_copy(
+            src_ref=src, dst_ref=dst, send_sem=ssem.at[i], recv_sem=rsem.at[i],
+            device_id={"head": hh, "dp": dd}, device_id_type=MESH,
+        )
+        copy.start()
+        copies.append(copy)
+        return copy
+
+    shifts = [(kx, kc) for kx in range(nx) for kc in range(2)]
+    apart = [s for s in shifts if s[0]] + [(0, 1)]
+    near = [(0, 1)] + [s for s in shifts if s[0]]
+
+    def ahead(s):
+        return ((x + s[0]) % nx) * 2 + (c + s[1]) % 2
+
+    def behind(s):
+        return (x + nx - s[0]) % nx, (c + s[1]) % 2
+
+    w_copy = pltpu.make_async_copy(w_hbm, w, lsem)
+    w_copy.start()
+    barrier = pltpu.get_barrier_semaphore()
+    for s in near:
+        pl.semaphore_signal(barrier, inc=1, device_id={"head": h, "dp": ahead(s)}, device_id_type=MESH)
+    for k in range(1, nh):
+        pl.semaphore_signal(barrier, inc=1, device_id={"head": (h + k) % nh, "dp": d}, device_id_type=MESH)
+    pl.semaphore_wait(barrier, nd + nh - 2)
+
+    def part(q):
+        return grad.at[:, pl.ds(pl.multiple_of(q * cols, 128), cols)]
+
+    swap = {}
+    for s in apart:
+        swap[s] = send(part(ahead(s)), g.at[b, x, c, a], h, ahead(s))
+    across, up = {}, {}
+
+    def spread(src, s):
+        qx, qc = behind(s)
+        up[s, 0] = send(src, g.at[b, qx, qc, a], other, d)
+        for k in range(1, na):
+            across[s, k] = send(src, g.at[b, qx, qc, a], ((a + k) % na) * 2 + b, d)
+
+    spread(part(d), (0, 0))
+    attn_x = {k: send(attn, blocks.at[x, c], h, ((x + k) % nx) * 2 + c) for k in range(1, nx)}
+    attn_c = send(attn, blocks.at[x, c], h, sibling)
+    g[b, x, c, a] = grad[:, pl.ds(pl.multiple_of(d * cols, 128), cols)]
+    for s in near:
+        swap[s].wait_recv()
+        qx, qc = behind(s)
+        spread(g.at[b, qx, qc, a], s)
+
+    def put(val, qx, qc):
+        val = (val.astype(F32) * gate[...]).astype(BF16).reshape(na, 2, rows, width)
+        for bb in range(2):
+            gated[bb, qx, qc] = val[:, bb]
+
+    put(attn[...], x, c)
+    attn_c.wait_recv()
+    put(blocks[x, 1 - c], x, 1 - c)
+    passed = {}
+    for k in range(1, nx):
+        attn_x[k].wait_recv()
+        qx = (x + nx - k) % nx
+        passed[k] = send(blocks.at[qx, c], blocks.at[qx, c], h, sibling)
+        put(blocks[qx, c], qx, c)
+    for k in range(1, nx):
+        passed[k].wait_recv()
+        qx = (x + nx - k) % nx
+        put(blocks[qx, 1 - c], qx, 1 - c)
+    w_copy.wait()
+
+    def project(bb, out):
+        @pl.loop(0, cols // TILE)
+        def _(t):
+            at = pl.ds(pl.multiple_of(t * TILE, TILE), TILE)
+            lhs = gated[bb].reshape(nd * na * rows, width)
+            res = jnp.dot(lhs, w[:, at], preferred_element_type=F32)
+            out[:, :, :, at] = res.astype(out.dtype).reshape(nd, na, rows, TILE)
+
+    project(1 - b, ps)
+
+    to_y = {}
+    order = [(q, k) for k in list(range(1, na)) + [0] for q in range(nd)]
+
+    def send_y(q, k):
+        to = (a + k) % na
+        to_y[q, k] = send(ps.at[q, to], ry.at[q, to], other, d)
+
+    pending = list(order)
+    for k in range(1, na):
+        for s in shifts:
+            across[s, k].wait_recv()
+            qx, qc = behind(s)
+            ref = g.at[b, qx, qc, (a + na - k) % na]
+            up[s, k] = send(ref, ref, other, d)
+            send_y(*pending.pop(0))
+    for q, k in pending:
+        send_y(q, k)
+    project(b, po)
+
+    to_z = {}
+    for k in range(1, na):
+        to = (a + k) % na
+        for q in range(nd):
+            to_y[q, k].wait_recv()
+            sz[q, to] = (po[q, to] + ry[q, to].astype(F32)).astype(BF16)
+            to_z[q, k] = send(sz.at[q, to], rz.at[k - 1, q], to * 2 + b, d)
+
+    for k in range(na):
+        for s in shifts:
+            up[s, k].wait_recv()
+
+    def back(cc, out):
+        @pl.loop(0, width // TILE)
+        def _(t):
+            at = pl.ds(pl.multiple_of(t * TILE, TILE), TILE)
+            lhs = g[:, :, cc].reshape(2 * nx * na * rows, cols)
+            res = lax.dot_general(lhs, w[at, :], (((1,), (1,)), ((), ())), preferred_element_type=F32)
+            out[:, :, :, :, at] = res.astype(out.dtype).reshape(2, nx, na, rows, TILE)
+
+    back(1 - c, bs)
+    pair = send(bs, br, h, sibling)
+    back(c, bo)
+    pair.wait_recv()
+    to_x = {}
+    for k in range(1, nx):
+        to = (x + k) % nx
+        bs2[k - 1] = (bo[:, to] + br[:, to].astype(F32)).astype(BF16)
+        to_x[k] = send(bs2.at[k - 1], br2.at[k - 1], h, to * 2 + c)
+
+    def out_copy(t, slot):
+        return pltpu.make_async_copy(
+            stage.at[slot], gw_hbm.at[pl.ds(pl.multiple_of(t * TILE, TILE), TILE), :], osem.at[slot])
+
+    tiles = width // TILE
+
+    @pl.loop(0, tiles)
+    def _(t):
+        slot = t % 2
+
+        @pl.when(t >= 2)
+        def _():
+            out_copy(t - 2, slot).wait()
+
+        at = pl.ds(pl.multiple_of(t * TILE, TILE), TILE)
+        lhs = gated[:, :, :, :, :, at].reshape(nd * nh * rows, TILE)
+        lhs = lhs.T
+        for n in range(0, cols, 2 * TILE):
+            rhs = g[:, :, :, :, :, n:n + 2 * TILE].reshape(nd * nh * rows, 2 * TILE)
+            stage[slot, :, n:n + 2 * TILE] = jnp.dot(lhs, rhs, preferred_element_type=F32)
+        out_copy(t, slot).start()
+
+    home = {}
+    for s in apart + [(0, 0)]:
+        q = ahead(s)
+        total = None
+        for k in range(1, na):
+            for qq in range(nd):
+                if s == apart[0]:
+                    to_z[qq, k].wait_recv()
+        if s == apart[0]:
+            for qq in range(nd):
+                to_y[qq, 0].wait_recv()
+        total = po[q, a] + ry[q, a].astype(F32)
+        for k in range(1, na):
+            total += rz[k - 1, q].astype(F32)
+        if s == (0, 0):
+            pj[d] = total.astype(BF16)
+        else:
+            fin[q] = total.astype(BF16)
+            home[s] = send(fin.at[q], pj.at[d], h, q)
+
+    for k in range(1, nx):
+        to_x[k].wait_recv()
+    total = bo[:, x] + br[:, x].astype(F32)
+    for k in range(1, nx):
+        total += br2[k - 1].astype(F32)
+    total = (total * gate[...].reshape(1, 1, 1, width)).astype(BF16)
+    for bb in range(2):
+        gattn[:, bb] = total[bb]
+
+    for s in apart:
+        home[s].wait_recv()
+    for q in range(nd):
+        proj[:, q * cols:(q + 1) * cols] = pj[q]
+    for t in range(max(tiles - 2, 0), tiles):
+        out_copy(t, t % 2).wait()
+    for copy in copies:
+        copy.wait_send()
+
+
+def fused(nh, nd, attn_out, col_gate, w_out, grad_out):
+    na, nx = nh // 2, nd // 2
+    rows, cols, width = grad_out.shape[0], w_out.shape[1], w_out.shape[0]
+    n_sems = 2 * nd + nx * 4 + nd * nh + nd * nh + nd * na * 2
+    vmem = pl.BlockSpec(memory_space=pltpu.VMEM)
+    hbm = pl.BlockSpec(memory_space=pl.ANY)
+    proj, gattn, gw = pl.pallas_call(
+        functools.partial(kernel, nh, nd),
+        out_shape=(
+            jax.ShapeDtypeStruct(grad_out.shape, BF16),
+            jax.ShapeDtypeStruct((na, 2, rows, width), BF16),
+            jax.ShapeDtypeStruct(w_out.shape, F32),
+        ),
+        in_specs=[vmem, vmem, vmem, hbm],
+        out_specs=(vmem, vmem, hbm),
+        scratch_shapes=[
+            pltpu.VMEM((nx, 2, nh * rows, width), BF16),
+            pltpu.VMEM((2, nx, 2, na, rows, width), BF16),
+            pltpu.VMEM(w_out.shape, BF16),
+            pltpu.VMEM((2, nx, 2, na, rows, cols), BF16),
+            pltpu.VMEM((nd, na, rows, cols), BF16),
+            pltpu.VMEM((nd, na, rows, cols), F32),
+            pltpu.VMEM((nd, na, rows, cols), BF16),
+            pltpu.VMEM((nd, na, rows, cols), BF16),
+            pltpu.VMEM((na - 1, nd, rows, cols), BF16),
+            pltpu.VMEM((nd, rows, cols), BF16),
+            pltpu.VMEM((nd, rows, cols), BF16),
+            pltpu.VMEM((2, nx, na, rows, width), BF16),
+            pltpu.VMEM((2, nx, na, rows, width), F32),
+            pltpu.VMEM((2, nx, na, rows, width), BF16),
+            pltpu.VMEM((nx - 1, 2, na, rows, width), BF16),
+            pltpu.VMEM((nx - 1, 2, na, rows, width), BF16),
+            pltpu.VMEM((2, TILE, cols), F32),
+            pltpu.SemaphoreType.DMA((n_sems,)),
+            pltpu.SemaphoreType.DMA((n_sems,)),
+            pltpu.SemaphoreType.DMA,
+            pltpu.SemaphoreType.DMA((2,)),
+        ],
+        compiler_params=pltpu.CompilerParams(
+            collective_id=0, has_side_effects=True, vmem_limit_bytes=VMEM_LIMIT
+        ),
+    )(attn_out, col_gate.reshape(1, width), grad_out, w_out)
+    return proj, gattn.reshape(attn_out.shape), gw
 
 
 def shards(attn_out, head_mask, gate_scale, w_out, grad_out):
@@ -9,8 +268,10 @@
     gate_vals = head_mask.astype(jnp.float32) * gate_scale
     width_each = attn_out.shape[1] // gate_vals.shape[0]
     col_gate = jnp.repeat(gate_vals, width_each)
+    rows, (width, cols) = grad_out.shape[0], w_out.shape
+    if rows % 16 == 0 and n_dp % 2 == 0 and n_head % 2 == 0 and min(n_dp, n_head) > 2 and width % TILE == 0 and cols % (2 * TILE) == 0:
+        return fused(n_head, n_dp, attn_out, col_gate, w_out, grad_out)
     gated = (attn_out.astype(jnp.float32) * col_gate[None, :]).astype(jnp.bfloat16)
-    rows, cols = grad_out.shape[0], w_out.shape[1]
     mine = lax.all_to_all(grad_out, "dp", 1, 0, tiled=True)
     every = lax.all_gather(mine.reshape(n_dp, rows, cols), "head", axis=1)
     grad_cols = every.reshape(n_dp * n_head * rows, cols)

time: 352 us -> 144 us (0.41)
  waiting for transfers between devices: 281 us -> 0 us
  Pallas kernels: 0 us -> 128 us
  matrix products: 24.1 us -> 0 us
  between operations: 13.8 us -> 0.64 us
  blocking collectives: 12.9 us -> 0 us
  starting transfers between devices: 3.64 us -> 0 us
    unnamed x5 -> x0, waiting for transfers between devices: 155 us -> none
    pallas_call x0 -> x1, Pallas kernels: none -> 128 us  [fused(): pl.pallas_call(functools.partial(kernel, nh, nd), out_shape=(jax.ShapeDty...]
    all_gather x2 -> x0, waiting for transfers between devices: 95.9 us -> none  [the longest x1 73.2 us: shards(): every = lax.all_gather(mine.reshape(n_dp, rows, cols), 'head', axis=1)]
    reduce_scatter x1 -> x0, waiting for transfers between devices: 29.7 us -> none  [shards(): lax.psum_scatter(back.astype(jnp.bfloat16), 'dp', scatter_dimension=0, ti...]
    dot_general x3 -> x0, matrix products: 24.1 us -> none  [the longest x1 9.33 us: shards(): jnp.dot(gated_all, w_out, preferred_element_type=jnp.float32)]
    all_to_all x1 -> x0, blocking collectives: 12.9 us -> none  [shards(): mine = lax.all_to_all(grad_out, 'dp', 1, 0, tiled=True)]
    unnamed x15 -> x3, local copies, waits for them, and re-layouts: 3.25 us -> 11.6 us
    all_to_all x4 -> x0, local copies, waits for them, and re-layouts: 5.67 us -> none  [the longest x2 3.4 us: shards(): lax.all_to_all(summed.reshape(n_dp * rows, cols), 'dp', 0, 1, tiled=True)]
  transfers between devices with their start and end apart: 5 -> 0, of which waited for: 4 -> 0; matrix products, arithmetic and copies ran while one was open for 3% -> 0% of each run, Pallas kernels for 0% -> 0%
where the time goes in v2:
time: 144 us; the launch traced here: 142 us
  Pallas kernels  128 us (89%)
  local copies, waits for them, and re-layouts  12.3 us (9%)
    pallas_call x1, Pallas kernels, fused(): pl.pallas_call(functools.partial(kernel, nh, nd), out_shape=(jax.ShapeDty...  128 us
    unnamed x3, local copies, waits for them, and re-layouts  11.6 us

profile of v2, /device:TPU:0, one launch (start us, length us, event | category | flops | bytes accessed | tf_op | source)
XLA Modules:
  0.0 141.6 jit_solution(12448136348152389994)
XLA Ops:
  0.6 0.7 convert_multiply_fusion
  1.3 0.7 broadcast_in_dim.3
  2.0 128.0 %shard_map.76 = (bf16[32,8192]{1,0:T(8,128)(2,1)}, bf16[4,2,32,1024]{3,2,1,0:T(8,128)(2,1)}, f32[1024,2048]{1,0:T(8,128)}) custom-call(bf16[256,1024]{1,0:T(8,128)(2,1)} %attn.1, f32[1,1024]{1,0:T(1,128)} %bitcast.3, bf16[32,8192]{1,0:T(8,128)(2,1)} %grad.1, bf16[1024,2048]{1,0:T(8,128)(2,1)} %w_hbm.1), custom_call_target="tpu_custom_call" | custom-call | tf_op jit(solution)/shard_map/pallas_call | solution.py:227
  130.0 1.9 %copy.11 = bf16[32,8192]{1,0:T(8,128)(2,1)} copy(bf16[32,8192]{1,0:T(8,128)(2,1)} %get-tuple-element.12) | data formatting | bytes 1048576
  131.8 1.9 %copy.12 = bf16[256,1024]{1,0:T(8,128)(2,1)} copy(bf16[256,1024]{1,0:T(8,128)(2,1)} %bitcast.2) | data formatting | bytes 1048576
  133.7 7.9 %copy.13 = f32[1024,2048]{1,0:T(8,128)} copy(f32[1024,2048]{1,0:T(8,128)} %get-tuple-element.14) | data formatting | bytes 16777216

commit v3 on v2

--- a/solution.py
+++ b/solution.py
@@ -10,6 +10,8 @@
 MESH = pl.DeviceIdType.MESH
 F32, BF16 = jnp.float32, jnp.bfloat16
 TILE = 256
+LEAD, EVERY = 3, 3
+N1, N2, N3 = 2, 1, 2
 VMEM_LIMIT = 62 * 1024 * 1024
 
 
@@ -78,6 +80,15 @@
         qx, qc = behind(s)
         spread(g.at[b, qx, qc, a], s)
 
+    def forward(s, k):
+        across[s, k].wait_recv()
+        qx, qc = behind(s)
+        ref = g.at[b, qx, qc, (a + na - k) % na]
+        up[s, k] = send(ref, ref, other, d)
+
+    for k in range(1, na):
+        forward((0, 0), k)
+
     def put(val, qx, qc):
         val = (val.astype(F32) * gate[...]).astype(BF16).reshape(na, 2, rows, width)
         for bb in range(2):
@@ -108,33 +119,41 @@
 
     project(1 - b, ps)
 
-    to_y = {}
-    order = [(q, k) for k in list(range(1, na)) + [0] for q in range(nd)]
-
-    def send_y(q, k):
-        to = (a + k) % na
-        to_y[q, k] = send(ps.at[q, to], ry.at[q, to], other, d)
-
-    pending = list(order)
-    for k in range(1, na):
-        for s in shifts:
-            across[s, k].wait_recv()
-            qx, qc = behind(s)
-            ref = g.at[b, qx, qc, (a + na - k) % na]
-            up[s, k] = send(ref, ref, other, d)
-            send_y(*pending.pop(0))
-    for q, k in pending:
-        send_y(q, k)
+    to_y, to_z = {}, {}
+    owners = apart + [(0, 0)]
+    order = [(s, k) for s in owners for k in list(range(1, na)) + [0]]
+
+    def send_y(s, k):
+        q, to = ahead(s), (a + k) % na
+        to_y[s, k] = send(ps.at[q, to], ry.at[q, to], other, d)
+
+    def send_z(s, k):
+        q, to = ahead(s), (a + k) % na
+        to_y[s, k].wait_recv()
+        if k:
+            sz[q, to] = (po[q, to] + ry[q, to].astype(F32)).astype(BF16)
+            to_z[s, k] = send(sz.at[q, to], rz.at[k - 1, q], to * 2 + b, d)
+
+    later = [(s, k) for s in near for k in range(1, na)]
+    ready, sent = list(order), []
+    for _ in range(LEAD):
+        sent.append(ready.pop(0))
+        send_y(*sent[-1])
     project(b, po)
-
-    to_z = {}
-    for k in range(1, na):
-        to = (a + k) % na
-        for q in range(nd):
-            to_y[q, k].wait_recv()
-            sz[q, to] = (po[q, to] + ry[q, to].astype(F32)).astype(BF16)
-            to_z[q, k] = send(sz.at[q, to], rz.at[k - 1, q], to * 2 + b, d)
-
+    for n, (s, k) in enumerate(later):
+        forward(s, k)
+        if EVERY and n % EVERY == EVERY - 1:
+            sent.append(ready.pop(0))
+            send_y(*sent[-1])
+    for s, k in ready:
+        send_y(s, k)
+    sent += ready
+
+    def drain(n):
+        for _ in range(min(n, len(sent))):
+            send_z(*sent.pop(0))
+
+    drain(LEAD)
     for k in range(na):
         for s in shifts:
             up[s, k].wait_recv()
@@ -149,7 +168,9 @@
 
     back(1 - c, bs)
     pair = send(bs, br, h, sibling)
+    drain(N1)
     back(c, bo)
+    drain(N2)
     pair.wait_recv()
     to_x = {}
     for k in range(1, nx):
@@ -157,47 +178,47 @@
         bs2[k - 1] = (bo[:, to] + br[:, to].astype(F32)).astype(BF16)
         to_x[k] = send(bs2.at[k - 1], br2.at[k - 1], h, to * 2 + c)
 
-    def out_copy(t, slot):
-        return pltpu.make_async_copy(
-            stage.at[slot], gw_hbm.at[pl.ds(pl.multiple_of(t * TILE, TILE), TILE), :], osem.at[slot])
-
-    tiles = width // TILE
-
-    @pl.loop(0, tiles)
-    def _(t):
-        slot = t % 2
-
-        @pl.when(t >= 2)
-        def _():
-            out_copy(t - 2, slot).wait()
-
-        at = pl.ds(pl.multiple_of(t * TILE, TILE), TILE)
-        lhs = gated[:, :, :, :, :, at].reshape(nd * nh * rows, TILE)
-        lhs = lhs.T
-        for n in range(0, cols, 2 * TILE):
-            rhs = g[:, :, :, :, :, n:n + 2 * TILE].reshape(nd * nh * rows, 2 * TILE)
-            stage[slot, :, n:n + 2 * TILE] = jnp.dot(lhs, rhs, preferred_element_type=F32)
-        out_copy(t, slot).start()
-
     home = {}
-    for s in apart + [(0, 0)]:
+
+    def finish(s):
         q = ahead(s)
-        total = None
-        for k in range(1, na):
-            for qq in range(nd):
-                if s == apart[0]:
-                    to_z[qq, k].wait_recv()
-        if s == apart[0]:
-            for qq in range(nd):
-                to_y[qq, 0].wait_recv()
         total = po[q, a] + ry[q, a].astype(F32)
         for k in range(1, na):
+            to_z[s, k].wait_recv()
             total += rz[k - 1, q].astype(F32)
         if s == (0, 0):
             pj[d] = total.astype(BF16)
         else:
             fin[q] = total.astype(BF16)
             home[s] = send(fin.at[q], pj.at[d], h, q)
+
+    def out_copy(t, slot):
+        return pltpu.make_async_copy(
+            stage.at[slot], gw_hbm.at[pl.ds(pl.multiple_of(t * TILE, TILE), TILE), :], osem.at[slot])
+
+    tiles = width // TILE
+
+    def weight_tile(t):
+        slot = t % 2
+        if t >= 2:
+            out_copy(t - 2, slot).wait()
+        at = pl.ds(t * TILE, TILE)
+        lhs = gated[:, :, :, :, :, at].reshape(nd * nh * rows, TILE).T
+
+        @pl.loop(0, cols // (2 * TILE))
+        def _(n):
+            to = pl.ds(pl.multiple_of(n * 2 * TILE, 2 * TILE), 2 * TILE)
+            rhs = g[:, :, :, :, :, to].reshape(nd * nh * rows, 2 * TILE)
+            stage[slot, :, to] = jnp.dot(lhs, rhs, preferred_element_type=F32)
+
+        out_copy(t, slot).start()
+
+    for t in range(tiles):
+        drain(N3)
+        weight_tile(t)
+    drain(len(sent))
+    for s in owners:
+        finish(s)
 
     for k in range(1, nx):
         to_x[k].wait_recv()

time: 144 us -> 127 us (0.88); the launches traced: 142 us -> 126 us
  Pallas kernels: 128 us -> 113 us
    pallas_call x1, Pallas kernels: 128 us -> 113 us  [fused(): pl.pallas_call(functools.partial(kernel, nh, nd), out_shape=(jax.ShapeDty...]
where the time goes in v3:
time: 127 us; the launch traced here: 126 us
  Pallas kernels  113 us (89%)
  local copies, waits for them, and re-layouts  12.3 us (10%)
    pallas_call x1, Pallas kernels, fused(): pl.pallas_call(functools.partial(kernel, nh, nd), out_shape=(jax.ShapeDty...  113 us
    unnamed x3, local copies, waits for them, and re-layouts  11.6 us

profile of v3, /device:TPU:0, one launch (start us, length us, event | category | flops | bytes accessed | tf_op | source)
XLA Modules:
  0.0 126.2 jit_solution(11984738553274445787)
XLA Ops:
  0.6 0.7 convert_multiply_fusion
  1.3 0.7 broadcast_in_dim.3
  2.0 112.6 %shard_map.76 = (bf16[32,8192]{1,0:T(8,128)(2,1)}, bf16[4,2,32,1024]{3,2,1,0:T(8,128)(2,1)}, f32[1024,2048]{1,0:T(8,128)}) custom-call(bf16[256,1024]{1,0:T(8,128)(2,1)} %attn.1, f32[1,1024]{1,0:T(1,128)} %bitcast.3, bf16[32,8192]{1,0:T(8,128)(2,1)} %grad.1, bf16[1024,2048]{1,0:T(8,128)(2,1)} %w_hbm.1), custom_call_target="tpu_custom_call" | custom-call | tf_op jit(solution)/shard_map/pallas_call | solution.py:248
  114.6 1.9 %copy.11 = bf16[32,8192]{1,0:T(8,128)(2,1)} copy(bf16[32,8192]{1,0:T(8,128)(2,1)} %get-tuple-element.12) | data formatting | bytes 1048576
  116.4 1.9 %copy.12 = bf16[256,1024]{1,0:T(8,128)(2,1)} copy(bf16[256,1024]{1,0:T(8,128)(2,1)} %bitcast.2) | data formatting | bytes 1048576
  118.3 7.9 %copy.13 = f32[1024,2048]{1,0:T(8,128)} copy(f32[1024,2048]{1,0:T(8,128)} %get-tuple-element.14) | data formatting | bytes 16777216
